TPU v7x, 128 devices: a whole 4x4x4 slice. The times are simulated.
128 devices in a mesh: dp: 2 (over z_lo), head: 8 (over z_hi, y), tensor: 8 (over x, core).
Axes of the slice: x: 4, y: 4, z: 4 (z_hi: 2, z_lo: 2; z = z_hi * 2 + z_lo), core: 2. Of those that a mesh axis runs over, the one named last changes fastest.
Arguments:
- tokens: bfloat16 [512, 8192], P('dp', 'tensor'), may hold values from -6 to 6
- cotangent: bfloat16 [512, 8192], P('dp', 'tensor'), may hold values from -6 to 6
- w_gate: bfloat16 [8192, 29568], P('tensor', 'head'), may hold values from -0.0625 to 0.0625
- w_up: bfloat16 [8192, 29568], P('tensor', 'head'), may hold values from -0.0625 to 0.0625
- w_down: bfloat16 [29568, 8192], P('head', 'tensor'), may hold values from -0.03125 to 0.03125
- common_down_factor: bfloat16 [8192, 64], P('tensor'), may hold values from -0.0625 to 0.0625
- head_up: bfloat16 [64, 64, 8192], P('head', None, 'tensor'), may hold values from -0.0625 to 0.0625
- routes: int32 [512, 1], P('dp'), may hold values from 0 to 63
Outputs:
- grad_x: bfloat16 [512, 8192], P(('dp', 'head'), 'tensor')
- grad_shared: float32 [8192, 64], P('tensor')
- up_head_gradients: float32 [64, 64, 8192], P('head', None, 'tensor')
Inputs may be any that keep to these rules, and one draw needn't show every extreme that they name: `routes`: each token names one adapter head; the loads are skewed.
All inputs are finite; a program needn't handle non-finite values.
Results may differ from a plain program's by a relative error of at most 0.015.
Values may be sent and summed in bfloat16 or wider, within the bound.
A program may use at most 128 MiB of HBM per device.

v0:
```python
import jax
import jax.numpy as jnp
from jax import lax
from jax.sharding import PartitionSpec as P

ADAPTER_SCALE = 2.0


def contract_last(left, right):
    return lax.dot_general(
        left, right, (((1,), (1,)), ((), ())), preferred_element_type=jnp.float32
    )


def local(tokens, cotangent, w_gate, w_up, w_down, common_down_factor, head_up, routes):
    tok_rows, d_cols = tokens.shape
    hidden_activation = w_gate.shape[1]
    reduced_activation = common_down_factor.shape[1]
    local_heads = head_up.shape[0]
    first_head = lax.axis_index("head") * local_heads
    assigned_mask = (
        routes == first_head + jnp.arange(local_heads, dtype=jnp.int32)[None, :]
    ).astype(jnp.float32)
    flat_heads = head_up.reshape(local_heads * reduced_activation, d_cols)
    gate_preactivation = jnp.dot(tokens, w_gate, preferred_element_type=jnp.float32)
    up_preactivation = jnp.dot(tokens, w_up, preferred_element_type=jnp.float32)
    returned_gradient = contract_last(cotangent, w_down)
    adapter_selectors = jnp.dot(tokens, common_down_factor, preferred_element_type=jnp.float32)
    head_separated = contract_last(cotangent, flat_heads).reshape(
        tok_rows, local_heads, reduced_activation
    )
    selector_gradient = ADAPTER_SCALE * jnp.sum(head_separated * assigned_mask[:, :, None], axis=1)
    partial = jnp.concatenate(
        [
            gate_preactivation.astype(jnp.bfloat16),
            up_preactivation.astype(jnp.bfloat16),
            returned_gradient.astype(jnp.bfloat16),
            adapter_selectors.astype(jnp.bfloat16),
            selector_gradient.astype(jnp.bfloat16),
        ],
        axis=1,
    )
    own_rows = lax.psum_scatter(partial, "tensor", scatter_dimension=0, tiled=True)
    gate_preactivation = own_rows[:, :hidden_activation].astype(jnp.float32)
    up_preactivation = own_rows[:, hidden_activation : 2 * hidden_activation].astype(jnp.float32)
    returned_gradient = own_rows[:, 2 * hidden_activation : 3 * hidden_activation].astype(
        jnp.float32
    )
    sig_gate = jax.nn.sigmoid(gate_preactivation)
    gate_gradient = (
        returned_gradient
        * up_preactivation
        * sig_gate
        * (1.0 + gate_preactivation * (1.0 - sig_gate))
    ).astype(jnp.bfloat16)
    up_gradient = (returned_gradient * gate_preactivation * sig_gate).astype(jnp.bfloat16)
    gathered = lax.all_gather(
        jnp.concatenate([gate_gradient, up_gradient, own_rows[:, 3 * hidden_activation :]], axis=1),
        "tensor",
        axis=0,
        tiled=True,
    )
    gate_gradient = gathered[:, :hidden_activation]
    up_gradient = gathered[:, hidden_activation : 2 * hidden_activation]
    adapter_selectors = gathered[
        :, 2 * hidden_activation : 2 * hidden_activation + reduced_activation
    ]
    selector_gradient = gathered[:, 2 * hidden_activation + reduced_activation :]
    ffn_part = (
        contract_last(gate_gradient, w_gate)
        + contract_last(up_gradient, w_up)
        + contract_last(selector_gradient, common_down_factor)
    )
    grad_x = lax.psum_scatter(
        ffn_part.astype(jnp.bfloat16), "head", scatter_dimension=0, tiled=True
    )
    selector_mask = (
        adapter_selectors[:, None, :] * assigned_mask[:, :, None].astype(jnp.bfloat16)
    ).reshape(tok_rows, local_heads * reduced_activation)
    head_contributions = ADAPTER_SCALE * lax.dot_general(
        selector_mask, cotangent, (((0,), (0,)), ((), ())), preferred_element_type=jnp.float32
    )
    up_head_gradients = lax.psum(
        head_contributions.reshape(local_heads, reduced_activation, d_cols).astype(jnp.bfloat16),
        "dp",
    ).astype(jnp.float32)
    shared_term = lax.dot_general(
        tokens, selector_gradient, (((0,), (0,)), ((), ())), preferred_element_type=jnp.float32
    )
    grad_shared = lax.psum(shared_term.astype(jnp.bfloat16), ("dp", "head")).astype(jnp.float32)
    return (grad_x, grad_shared, up_head_gradients)


def solution(mesh):
    placed = (
        P("dp", "tensor"),
        P("dp", "tensor"),
        P("tensor", "head"),
        P("tensor", "head"),
        P("head", "tensor"),
        P("tensor", None),
        P("head", None, "tensor"),
        P("dp", None),
    )
    return jax.shard_map(
        local,
        mesh=mesh,
        in_specs=placed,
        out_specs=(P(("dp", "head"), "tensor"), P("tensor", None), P("head", None, "tensor")),
        check_vma=False,
    )
```

profile of v0, /device:TPU:0, one launch (start us, length us, event | category | flops | bytes accessed | tf_op | source)
XLA Modules:
  0.0 327.6 jit_solution(7032396311072623166)
XLA Ops:
  7.2 0.0 copy-start
  7.2 0.0 reduce-scatter.7.cloned.1.call-start
  7.2 0.8 fusion.27
  8.1 0.0 copy-start.1
  8.1 0.0 copy-start.5
  8.1 0.0 slice-start
  8.1 6.9 %fusion.2 = bf16[256,11216]{0,1:T(8,128)(2,1)} fusion(bf16[256,1024]{1,0:T(8,128)(2,1)} %param.8, bf16[1024,3696]{0,1:T(8,128)(2,1)} %param.10), kind=kOutput, calls=%fused_computation.5 | convolution fusion | flops 1938714624 | bytes 9986048 | tf_op jit(solution)/shard_map/dot_general | solution.py:25
  15.0 0.0 copy-done.1
  15.0 0.0 copy-done.5
  15.0 0.0 copy-start.2
  15.0 0.0 slice-start.1
  15.0 3.5 %fusion.1 = bf16[256,11216]{0,1:T(8,128)(2,1)} fusion(bf16[256,11216]{0,1:T(8,128)(2,1)} %fusion.2, bf16[256,1024]{1,0:T(8,128)(2,1)S(1)} %copy-done.1, bf16[1024,3696]{0,1:T(8,128)(2,1)S(1)} %copy-done.5), kind=kOutput, calls=%fused_computation.3 | convolution fusion | flops 1938714624 | bytes 9986048 | tf_op jit(solution)/shard_map/dot_general | solution.py:26
  18.5 0.0 copy-done
  18.5 0.0 copy-done.2
  18.5 0.5 fusion.11
  19.0 0.0 slice-done
  19.0 0.0 slice-done.1
  19.0 0.0 copy-start.3
  19.0 3.4 %fusion = bf16[256,11216]{0,1:T(8,128)(2,1)} fusion(bf16[256,11216]{0,1:T(8,128)(2,1)} %fusion.1, bf16[256,1024]{1,0:T(8,128)(2,1)S(1)} %copy-done.2, bf16[3696,1024]{1,0:T(8,128)(2,1)S(1)} %bitcast.28), kind=kOutput, calls=%fused_computation.1 | convolution fusion | flops 1938714624 | bytes 9986048 | tf_op jit(solution)/shard_map/dot_general | solution.py:10
  22.5 0.0 copy-done.3
  22.5 0.9 fusion.13
  23.4 0.6 fusion.26
  24.0 8.5 %copy.22 = bf16[256,11216]{1,0:T(8,128)(2,1)} copy(bf16[256,11216]{0,1:T(8,128)(2,1)} %fusion.26) | data formatting | bytes 11485184
  32.4 0.0 reduce-scatter.7.cloned.1.call-update
  32.5 0.0 all-gather.2.cloned.1.call-start
  32.5 43.7 %reduce-scatter.7.cloned.1.call-done = bf16[32,11216]{1,0:T(8,128)(2,1)} async-done(((bf16[256,11216]{1,0:T(8,128)(2,1)}), bf16[32,11216]{1,0:T(8,128)(2,1)}) %reduce-scatter.7.cloned.1.call-update) | async-done | bytes 717840 | tf_op jit(solution)/shard_map/reduce_scatter | solution.py:43
  76.2 0.8 slice.35
  77.0 1.5 fusion.23
  78.6 1.0 concatenate.7
  79.6 0.0 all-gather.2.cloned.1.call-update
  79.6 0.0 all-reduce.3.cloned.1.call-start
  79.7 30.3 %all-gather.2.cloned.1.call-done = bf16[256,7520]{1,0:T(8,128)(2,1)} async-done(((bf16[32,7520]{1,0:T(8,128)(2,1)}), bf16[256,7520]{1,0:T(8,128)(2,1)}) %all-gather.2.cloned.1.call-update) | async-done | bytes 3850256 | tf_op jit(solution)/shard_map/all_gather | solution.py:57
  110.0 1.0 slice.39
  111.0 0.1 copy.21
  111.1 1.8 fusion.12
  112.9 0.0 all-reduce.3.cloned.1.call-update
  112.9 0.0 all-reduce.5.cloned.1.call-start
  113.0 1.4 multiply_convert_fusion
  114.4 0.0 all-reduce.5.cloned.1.call-update
  114.4 0.2 reduce-scatter.5.cloned.1.call-start
  114.7 0.0 copy-start.4
  114.7 6.1 %fusion.3 = f32[256,1024]{1,0:T(8,128)S(1)} fusion(bf16[1024,3696]{0,1:T(8,128)(2,1)} %param.11, bf16[256,7520]{1,0:T(8,128)(2,1)} %all-gather.2.cloned.1.call-done), kind=kOutput, calls=%fused_computation.7 | convolution fusion | flops 1937768448 | bytes 10518528 | tf_op jit(solution)/shard_map/dot_general | solution.py:10
  120.8 0.0 copy-done.4
  120.8 5.5 %fusion.7 = f32[256,1024]{1,0:T(8,128)S(1)} fusion(f32[256,1024]{1,0:T(8,128)S(1)} %fusion.3, bf16[1024,3696]{0,1:T(8,128)(2,1)} %param.10, bf16[256,7520]{1,0:T(8,128)(2,1)S(1)} %copy-done.4), kind=kOutput, calls=%fused_computation.12 | convolution fusion | flops 1938030592 | bytes 11567104 | tf_op jit(solution)/shard_map/dot_general | solution.py:10
  126.3 1.1 fusion.10
  127.5 0.0 reduce-scatter.5.cloned.1.call-update
  127.5 68.6 %all-reduce.3.cloned.1.call-done = bf16[1024,64]{0,1:T(8,128)(2,1)} async-done(((bf16[1024,64]{0,1:T(8,128)(2,1)}), bf16[1024,64]{0,1:T(8,128)(2,1)}) %all-reduce.3.cloned.1.call-update) | async-done | bytes 131088 | tf_op jit(solution)/shard_map/psum | solution.py:90
  196.1 1.6 convert_element_type.83
  197.8 47.5 %all-reduce.5.cloned.1.call-done = bf16[8,64,1024]{2,1,0:T(8,128)(2,1)} async-done(((bf16[8,64,1024]{2,1,0:T(8,128)(2,1)}), bf16[8,64,1024]{2,1,0:T(8,128)(2,1)}) %all-reduce.5.cloned.1.call-update) | async-done | bytes 1048592 | tf_op jit(solution)/shard_map/psum | solution.py:83
  245.2 2.8 convert_element_type.87
  248.0 73.1 %reduce-scatter.5.cloned.1.call-done = bf16[32,1024]{1,0:T(8,128)(2,1)} async-done(((bf16[256,1024]{1,0:T(8,128)(2,1)}), bf16[32,1024]{1,0:T(8,128)(2,1)}) %reduce-scatter.5.cloned.1.call-update) | async-done | bytes 65552 | tf_op jit(solution)/shard_map/reduce_scatter | solution.py:74
  (3 shorter events, 0.0 us)
Async XLA Ops:
  7.2 11.3 %copy-start = (bf16[8,64,1024]{2,1,0:T(8,128)(2,1)S(1)}, bf16[8,64,1024]{2,1,0:T(8,128)(2,1)}, u32[]{:S(2)}) copy-start(bf16[8,64,1024]{2,1,0:T(8,128)(2,1)} %param.14) | copy-start | bytes 3145732
  7.2 69.1 %reduce-scatter.7.cloned.1.call-start = ((), (), s32[]{:S(2)}) async-start(), calls=%async_computation.6 | async-start | bytes 6488064 | tf_op jit(solution)/shard_map/reduce_scatter | solution.py:43
  8.1 6.9 %copy-start.1 = (bf16[256,1024]{1,0:T(8,128)(2,1)S(1)}, bf16[256,1024]{1,0:T(8,128)(2,1)}, u32[]{:S(2)}) copy-start(bf16[256,1024]{1,0:T(8,128)(2,1)} %param.8) | copy-start | bytes 1572868
  8.1 6.9 %copy-start.5 = (bf16[1024,3696]{0,1:T(8,128)(2,1)S(1)}, bf16[1024,3696]{0,1:T(8,128)(2,1)}, u32[]{:S(2)}) copy-start(bf16[1024,3696]{0,1:T(8,128)(2,1)} %param.11) | copy-start | bytes 22708228
  8.1 10.9 %slice-start = ((s8[7569408]{0:T(1024)(128)(4,1)}), s8[4194304]{0:T(1024)(128)(4,1)S(1)}, s32[]{:S(2)}) async-start(s8[7569408]{0:T(1024)(128)(4,1)} %bitcast.27), calls=%async_computation.7 | async-start | bytes 8388608
  15.0 3.5 %copy-start.2 = (bf16[256,1024]{1,0:T(8,128)(2,1)S(1)}, bf16[256,1024]{1,0:T(8,128)(2,1)}, u32[]{:S(2)}) copy-start(bf16[256,1024]{1,0:T(8,128)(2,1)} %param.9) | copy-start | bytes 1572868
  15.0 4.0 %slice-start.1 = ((s8[7569408]{0:T(1024)(128)(4,1)}), s8[3375104]{0:T(1024)(128)(4,1)S(1)}, s32[]{:S(2)}) async-start(s8[7569408]{0:T(1024)(128)(4,1)} %bitcast.27), calls=%async_computation.8 | async-start | bytes 6750208
  19.0 3.5 %copy-start.3 = (bf16[1024,64]{0,1:T(8,128)(2,1)S(1)}, bf16[1024,64]{0,1:T(8,128)(2,1)}, u32[]{:S(2)}) copy-start(bf16[1024,64]{0,1:T(8,128)(2,1)} %param.13) | copy-start | bytes 393220
  32.5 77.5 %all-gather.2.cloned.1.call-start = ((), (), s32[]{:S(2)}) async-start(), calls=%async_computation.2 | async-start | bytes 4349952 | tf_op jit(solution)/shard_map/all_gather | solution.py:57
  79.6 116.5 %all-reduce.3.cloned.1.call-start = ((), (), s32[]{:S(2)}) async-start(), calls=%async_computation.4 | async-start | bytes 262144 | tf_op jit(solution)/shard_map/psum | solution.py:90
  112.9 132.3 %all-reduce.5.cloned.1.call-start = ((), (), s32[]{:S(2)}) async-start(), calls=%async_computation.5 | async-start | bytes 2097152 | tf_op jit(solution)/shard_map/psum | solution.py:83
  114.4 206.7 %reduce-scatter.5.cloned.1.call-start = ((), (), s32[]{:S(2)}) async-start(), calls=%async_computation.3 | async-start | bytes 589824 | tf_op jit(solution)/shard_map/reduce_scatter | solution.py:74
  114.7 6.1 %copy-start.4 = (bf16[256,7520]{1,0:T(8,128)(2,1)S(1)}, bf16[256,7520]{1,0:T(8,128)(2,1)}, u32[]{:S(2)}) copy-start(bf16[256,7520]{1,0:T(8,128)(2,1)} %all-gather.2.cloned.1.call-done) | copy-start | bytes 11550724
Sparse Core Ops, SparseCore 0:
  32.6 43.6 reduce-scatter.6
  79.7 30.2 all-gather.1
  113.8 82.3 all-reduce.2
  199.2 46.0 all-reduce.4
  249.2 71.8 reduce-scatter.4
where the time goes:
time: 328 us
  waiting for transfers between devices  263 us (80%)
  matrix products  31.2 us (10%)
  between operations  13.9 us (4%)
  local copies, waits for them, and re-layouts  11.4 us (3%)
  other arithmetic  7.4 us (2%)
    reduce_scatter x1, waiting for transfers between devices, local(): lax.psum_scatter(ffn_part.astype(jnp.bfloat16), 'head', scatter_dimension...  73.1 us
    psum x1, waiting for transfers between devices, local(): lax.psum(shared_term.astype(jnp.bfloat16), ('dp', 'head'))  68.6 us
    psum x1, waiting for transfers between devices, local(): lax.psum(head_contributions.reshape(local_heads, reduced_activation, d_co...  47.5 us
    reduce_scatter x1, waiting for transfers between devices, local(): lax.psum_scatter(partial, 'tensor', scatter_dimension=0, tiled=True)  43.7 us
    all_gather x1, waiting for transfers between devices, local(): lax.all_gather(jnp.concatenate([gate_gradient, up_gradient, own_rows[:, 3...  30.3 us
    dot_general x5, matrix products, contract_last(): lax.dot_general(left, right, (((1,), (1,)), ((), ())), preferred_element_...  16.7 us
    unnamed x17, local copies, waits for them, and re-layouts  8.5 us
    dot_general x1, matrix products, local(): jnp.dot(tokens, w_gate, preferred_element_type=jnp.float32)  6.88 us
  transfers between devices with their start and end apart: 5, of which 5 were waited for; matrix products, arithmetic and copies ran while one was open for 6% of the time, Pallas kernels for 0%

commit v1 on v0

--- a/solution.py
+++ b/solution.py
@@ -4,6 +4,16 @@
 from jax.sharding import PartitionSpec as P
 
 ADAPTER_SCALE = 2.0
+
+
+def finish_halves_in(row_data, k_dim):
+    row_data = jnp.moveaxis(row_data, 0, k_dim)
+    current_value = row_data.shape
+    return row_data.reshape(
+        *current_value[:k_dim],
+        current_value[k_dim] * current_value[k_dim + 1],
+        *current_value[k_dim + 2 :]
+    )
 
 
 def contract_last(left, right):
@@ -54,11 +64,29 @@
         * (1.0 + gate_preactivation * (1.0 - sig_gate))
     ).astype(jnp.bfloat16)
     up_gradient = (returned_gradient * gate_preactivation * sig_gate).astype(jnp.bfloat16)
-    gathered = lax.all_gather(
+
+    def launch_row(x_local, along_axis, where_dim):
+        degree = jax.lax.axis_size(along_axis)
+        store = [(it, (it + 1) % degree) for it in range(degree)]
+        pile = [(jj, hop_no) for hop_no, jj in store]
+        latest, shaped = ([], [])
+        for ii in range(degree - 1):
+            if ii % 2 == 0:
+                latest.append(
+                    jax.lax.ppermute(latest[-1] if latest else x_local, along_axis, store)
+                )
+            else:
+                shaped.append(jax.lax.ppermute(shaped[-1] if shaped else x_local, along_axis, pile))
+        value_now = jnp.stack([*latest[::-1], x_local, *shaped], axis=0)
+        outcome_arr = jax.lax.axis_index(along_axis)
+        long_array = outcome_arr - len(latest)
+        value_now = value_now[(jnp.arange(degree) - long_array) % degree]
+        return finish_halves_in(value_now, where_dim)
+
+    gathered = launch_row(
         jnp.concatenate([gate_gradient, up_gradient, own_rows[:, 3 * hidden_activation :]], axis=1),
         "tensor",
-        axis=0,
-        tiled=True,
+        0,
     )
     gate_gradient = gathered[:, :hidden_activation]
     up_gradient = gathered[:, hidden_activation : 2 * hidden_activation]

time: 328 us -> 350 us (1.067)
  local copies, waits for them, and re-layouts: 11.4 us -> 27.9 us
  starting transfers between devices: 0.39 us -> 8.73 us
    all_gather x1 -> x0, waiting for transfers between devices: 30.3 us -> none  [local(): lax.all_gather(jnp.concatenate([gate_gradient, up_gradient, own_rows[:, 3...]
    ppermute x0 -> x7, waiting for transfers between devices: none -> 28.8 us  [the longest x4 28.6 us: launch_row(): jax.lax.ppermute(latest[-1] if latest else x_local, along_axis, store)]
    unnamed x17 -> x26, local copies, waits for them, and re-layouts: 8.5 us -> 20 us
    ppermute x0 -> x7, starting transfers between devices: none -> 8.38 us  [the longest x3 8.36 us: launch_row(): jax.lax.ppermute(shaped[-1] if shaped else x_local, along_axis, pile)]
    gather x0 -> x1, local copies, waits for them, and re-layouts: none -> 4.87 us  [launch_row(): value_now = value_now[(jnp.arange(degree) - long_array) % degree]]
  transfers between devices with their start and end apart: 5 -> 11, of which waited for: 5 -> 9; matrix products, arithmetic and copies ran while one was open for 6% -> 8% of each run, Pallas kernels for 0% -> 0%
where the time goes in v1:
time: 350 us; the launch traced here: 349 us
  waiting for transfers between devices  260 us (74%)
  matrix products  31.2 us (9%)
  local copies, waits for them, and re-layouts  27.9 us (8%)
  between operations  13.9 us (4%)
  starting transfers between devices  8.73 us (2%)
  other arithmetic  7.42 us (2%)
    reduce_scatter x1, waiting for transfers between devices, local(): lax.psum_scatter(ffn_part.astype(jnp.bfloat16), 'head', scatter_dimension...  73.1 us
    psum x1, waiting for transfers between devices, local(): lax.psum(shared_term.astype(jnp.bfloat16), ('dp', 'head'))  66.7 us
    psum x1, waiting for transfers between devices, local(): lax.psum(head_contributions.reshape(local_heads, reduced_activation, d_co...  47.6 us
    reduce_scatter x1, waiting for transfers between devices, local(): lax.psum_scatter(partial, 'tensor', scatter_dimension=0, tiled=True)  43.7 us
    ppermute x4, waiting for transfers between devices, launch_row(): jax.lax.ppermute(latest[-1] if latest else x_local, along_axis, store)  28.6 us
    unnamed x26, local copies, waits for them, and re-layouts  20 us
    dot_general x5, matrix products, contract_last(): lax.dot_general(left, right, (((1,), (1,)), ((), ())), preferred_element_...  16.7 us
    ppermute x3, starting transfers between devices, launch_row(): jax.lax.ppermute(shaped[-1] if shaped else x_local, along_axis, pile)  8.36 us
  transfers between devices with their start and end apart: 11, of which 9 were waited for; matrix products, arithmetic and copies ran while one was open for 8% of the time, Pallas kernels for 0%

profile of v1, /device:TPU:0, one launch (start us, length us, event | category | flops | bytes accessed | tf_op | source)
XLA Modules:
  0.0 349.1 jit_solution(14138412070372311462)
XLA Ops:
  7.2 0.0 copy-start
  7.2 0.0 reduce-scatter.7.cloned.1.call-start
  7.2 0.8 fusion.27
  8.1 6.9 %fusion.2 = bf16[256,11216]{0,1:T(8,128)(2,1)} fusion(bf16[256,1024]{1,0:T(8,128)(2,1)} %param.8, bf16[1024,3696]{0,1:T(8,128)(2,1)} %param.10), kind=kOutput, calls=%fused_computation.6 | convolution fusion | flops 1938714624 | bytes 9986048 | tf_op jit(solution)/shard_map/dot_general | solution.py:35
  15.0 0.0 copy-done.2
  15.0 0.0 copy-done.6
  15.0 0.0 slice-start.1
  15.0 3.5 %fusion.1 = bf16[256,11216]{0,1:T(8,128)(2,1)} fusion(bf16[256,11216]{0,1:T(8,128)(2,1)} %fusion.2, bf16[256,1024]{1,0:T(8,128)(2,1)S(1)} %copy-done.2, bf16[1024,3696]{0,1:T(8,128)(2,1)S(1)} %copy-done.6), kind=kOutput, calls=%fused_computation.4 | convolution fusion | flops 1938714624 | bytes 9986048 | tf_op jit(solution)/shard_map/dot_general | solution.py:36
  18.5 0.0 copy-done
  18.5 0.5 fusion.11
  19.0 0.0 copy-start.4
  19.0 3.4 fusion
  22.4 0.0 copy-done.4
  22.4 0.9 fusion.13
  23.3 0.6 fusion.26
  23.9 8.4 %copy.23 = bf16[256,11216]{1,0:T(8,128)(2,1)} copy(bf16[256,11216]{0,1:T(8,128)(2,1)} %fusion.26) | data formatting | bytes 11485184
  32.3 0.0 reduce-scatter.7.cloned.1.call-update
  32.4 0.0 all-reduce.3.cloned.1.call-start
  32.4 43.7 %reduce-scatter.7.cloned.1.call-done = bf16[32,11216]{1,0:T(8,128)(2,1)} async-done(((bf16[256,11216]{1,0:T(8,128)(2,1)}), bf16[32,11216]{1,0:T(8,128)(2,1)}) %reduce-scatter.7.cloned.1.call-update) | async-done | bytes 717840 | tf_op jit(solution)/shard_map/reduce_scatter | solution.py:53
  76.1 1.5 fusion.23
  77.6 0.8 slice.37
  78.4 0.3 concatenate.7
  78.7 0.0 collective-permute-start
  78.7 9.4 %collective-permute-done = bf16[32,7520]{1,0:T(8,128)(2,1)S(1)} collective-permute-done((bf16[32,7520]{1,0:T(8,128)(2,1)S(1)}, bf16[32,7520]{1,0:T(8,128)(2,1)S(1)}, u32[]{:S(2)}, u32[]{:S(2)}) %collective-permute-start) | collective-permute-done | bytes 481312 | tf_op jit(solution)/shard_map/ppermute | solution.py:76
  88.1 0.0 collective-permute-start.1
  88.1 3.0 collective-permute-start.4
  91.0 6.4 %collective-permute-done.1 = bf16[32,7520]{1,0:T(8,128)(2,1)S(1)} collective-permute-done((bf16[32,7520]{1,0:T(8,128)(2,1)S(1)}, bf16[32,7520]{1,0:T(8,128)(2,1)S(1)}, u32[]{:S(2)}, u32[]{:S(2)}) %collective-permute-start.1) | collective-permute-done | bytes 481312 | tf_op jit(solution)/shard_map/ppermute | solution.py:76
  97.5 0.0 collective-permute-start.2
  97.5 0.0 collective-permute-done.4
  97.5 0.8 copy-done.5
  98.2 2.3 collective-permute-start.5
  100.5 6.4 %collective-permute-done.2 = bf16[32,7520]{1,0:T(8,128)(2,1)} collective-permute-done((bf16[32,7520]{1,0:T(8,128)(2,1)S(1)}, bf16[32,7520]{1,0:T(8,128)(2,1)}, u32[]{:S(2)}, u32[]{:S(2)}) %collective-permute-start.2) | collective-permute-done | bytes 481312 | tf_op jit(solution)/shard_map/ppermute | solution.py:76
  106.9 0.0 collective-permute-start.3
  107.0 0.1 collective-permute-done.5
  107.1 3.1 collective-permute-start.6
  110.2 6.4 %collective-permute-done.3 = bf16[32,7520]{1,0:T(8,128)(2,1)} collective-permute-done((bf16[32,7520]{1,0:T(8,128)(2,1)}, bf16[32,7520]{1,0:T(8,128)(2,1)}, u32[]{:S(2)}, u32[]{:S(2)}) %collective-permute-start.3) | collective-permute-done | bytes 481312 | tf_op jit(solution)/shard_map/ppermute | solution.py:76
  116.6 1.8 bitcast_dynamic-update-slice_fusion.7
  118.5 1.8 bitcast_dynamic-update-slice_fusion.6
  120.3 1.9 bitcast_dynamic-update-slice_fusion.5
  122.2 0.8 bitcast_dynamic-update-slice_fusion.4
  123.0 0.8 bitcast_dynamic-update-slice_fusion.3
  123.8 1.8 bitcast_dynamic-update-slice_fusion.2
  125.6 1.8 bitcast_dynamic-update-slice_fusion.1
  127.5 0.0 collective-permute-done.6
  127.5 0.8 bitcast_dynamic-update-slice_fusion
  128.3 4.9 %gather_fusion = bf16[8,32,7520]{2,1,0:T(8,128)(2,1)} fusion(bf16[8,32,7520]{2,1,0:T(8,128)(2,1)} %bitcast_dynamic-update-slice_fusion, s32[1024]{0:T(1024)S(1)} %pad_clamp_fusion), kind=kCustom, calls=%fused_computation | custom fusion | bytes 7700512 | tf_op jit(solution)/shard_map/gather | solution.py:83
  133.2 1.0 slice.41
  134.2 1.8 fusion.12
  136.0 0.1 copy.22
  136.1 0.0 all-reduce.3.cloned.1.call-update
  136.1 0.0 all-reduce.5.cloned.1.call-start
  136.2 1.4 multiply_convert_fusion
  137.6 0.0 all-reduce.5.cloned.1.call-update
  137.6 0.2 reduce-scatter.5.cloned.1.call-start
  137.8 0.0 copy-start.1
  137.8 6.1 %fusion.3 = f32[256,1024]{1,0:T(8,128)S(1)} fusion(bf16[1024,3696]{0,1:T(8,128)(2,1)} %param.11, bf16[256,7520]{1,0:T(8,128)(2,1)} %bitcast.45), kind=kOutput, calls=%fused_computation.8 | convolution fusion | flops 1937768448 | bytes 10518528 | tf_op jit(solution)/shard_map/dot_general | solution.py:20
  144.0 5.5 %fusion.7 = f32[256,1024]{1,0:T(8,128)S(1)} fusion(f32[256,1024]{1,0:T(8,128)S(1)} %fusion.3, bf16[1024,3696]{0,1:T(8,128)(2,1)} %param.10, bf16[256,7520]{1,0:T(8,128)(2,1)S(1)} %bitcast.46), kind=kOutput, calls=%fused_computation.13 | convolution fusion | flops 1938030592 | bytes 11567104 | tf_op jit(solution)/shard_map/dot_general | solution.py:20
  149.5 1.2 fusion.10
  150.6 0.0 reduce-scatter.5.cloned.1.call-update
  150.7 66.7 %all-reduce.3.cloned.1.call-done = bf16[1024,64]{0,1:T(8,128)(2,1)} async-done(((bf16[1024,64]{0,1:T(8,128)(2,1)}), bf16[1024,64]{0,1:T(8,128)(2,1)}) %all-reduce.3.cloned.1.call-update) | async-done | bytes 131088 | tf_op jit(solution)/shard_map/psum | solution.py:118
  217.4 1.6 convert_element_type.83
  219.0 47.6 %all-reduce.5.cloned.1.call-done = bf16[8,64,1024]{2,1,0:T(8,128)(2,1)} async-done(((bf16[8,64,1024]{2,1,0:T(8,128)(2,1)}), bf16[8,64,1024]{2,1,0:T(8,128)(2,1)}) %all-reduce.5.cloned.1.call-update) | async-done | bytes 1048592 | tf_op jit(solution)/shard_map/psum | solution.py:111
  266.6 2.8 convert_element_type.87
  269.4 73.1 %reduce-scatter.5.cloned.1.call-done = bf16[32,1024]{1,0:T(8,128)(2,1)} async-done(((bf16[256,1024]{1,0:T(8,128)(2,1)}), bf16[32,1024]{1,0:T(8,128)(2,1)}) %reduce-scatter.5.cloned.1.call-update) | async-done | bytes 65552 | tf_op jit(solution)/shard_map/reduce_scatter | solution.py:102
  (14 shorter events, 0.1 us)
Async XLA Ops:
  7.2 11.3 %copy-start = (bf16[8,64,1024]{2,1,0:T(8,128)(2,1)S(1)}, bf16[8,64,1024]{2,1,0:T(8,128)(2,1)}, u32[]{:S(2)}) copy-start(bf16[8,64,1024]{2,1,0:T(8,128)(2,1)} %param.14) | copy-start | bytes 3145732
  7.2 68.9 %reduce-scatter.7.cloned.1.call-start = ((), (), s32[]{:S(2)}) async-start(), calls=%async_computation.5 | async-start | bytes 6488064 | tf_op jit(solution)/shard_map/reduce_scatter | solution.py:53
  8.1 6.9 %copy-start.2 = (bf16[256,1024]{1,0:T(8,128)(2,1)S(1)}, bf16[256,1024]{1,0:T(8,128)(2,1)}, u32[]{:S(2)}) copy-start(bf16[256,1024]{1,0:T(8,128)(2,1)} %param.8) | copy-start | bytes 1572868
  8.1 6.9 %copy-start.6 = (bf16[1024,3696]{0,1:T(8,128)(2,1)S(1)}, bf16[1024,3696]{0,1:T(8,128)(2,1)}, u32[]{:S(2)}) copy-start(bf16[1024,3696]{0,1:T(8,128)(2,1)} %param.11) | copy-start | bytes 22708228
  8.1 10.9 %slice-start = ((s8[7569408]{0:T(1024)(128)(4,1)}), s8[4194304]{0:T(1024)(128)(4,1)S(1)}, s32[]{:S(2)}) async-start(s8[7569408]{0:T(1024)(128)(4,1)} %bitcast.51), calls=%async_computation.6 | async-start | bytes 8388608
  15.0 3.5 %copy-start.3 = (bf16[256,1024]{1,0:T(8,128)(2,1)S(1)}, bf16[256,1024]{1,0:T(8,128)(2,1)}, u32[]{:S(2)}) copy-start(bf16[256,1024]{1,0:T(8,128)(2,1)} %param.9) | copy-start | bytes 1572868
  15.0 4.0 %slice-start.1 = ((s8[7569408]{0:T(1024)(128)(4,1)}), s8[3375104]{0:T(1024)(128)(4,1)S(1)}, s32[]{:S(2)}) async-start(s8[7569408]{0:T(1024)(128)(4,1)} %bitcast.51), calls=%async_computation.7 | async-start | bytes 6750208
  19.0 3.4 copy-start.4
  32.4 185.1 %all-reduce.3.cloned.1.call-start = ((), (), s32[]{:S(2)}) async-start(), calls=%async_computation.3 | async-start | bytes 262144 | tf_op jit(solution)/shard_map/psum | solution.py:118
  78.7 9.4 %collective-permute-start = (bf16[32,7520]{1,0:T(8,128)(2,1)S(1)}, bf16[32,7520]{1,0:T(8,128)(2,1)S(1)}, u32[]{:S(2)}, u32[]{:S(2)}) collective-permute-start(bf16[32,7520]{1,0:T(8,128)(2,1)S(1)} %concatenate.7), channel_id=1, source_target_pairs={{0,1},{1,2},{2,3},{3,4},{4,5},{5,6},{6,7},{7,0},{8,9},{9,10},{10,1... | collective-permute-start | bytes 1443848 | tf_op jit(solution)/shard_map/ppermute | solution.py:76
  88.1 9.4 %collective-permute-start.1 = (bf16[32,7520]{1,0:T(8,128)(2,1)S(1)}, bf16[32,7520]{1,0:T(8,128)(2,1)S(1)}, u32[]{:S(2)}, u32[]{:S(2)}) collective-permute-start(bf16[32,7520]{1,0:T(8,128)(2,1)S(1)} %collective-permute-done), channel_id=1, source_target_pairs={{0,1},{1,2},{2,3},{3,4},{4,5},{5,6},{6,7},{7,0},{8,9},{9,10},{10,1... | collective-permute-start | bytes 1443848 | tf_op jit(solution)/shard_map/ppermute | solution.py:76
  88.1 9.4 %collective-permute-start.4 = (bf16[32,7520]{1,0:T(8,128)(2,1)S(1)}, bf16[32,7520]{1,0:T(8,128)(2,1)}, u32[]{:S(2)}, u32[]{:S(2)}) collective-permute-start(bf16[32,7520]{1,0:T(8,128)(2,1)S(1)} %concatenate.7), channel_id=1, source_target_pairs={{1,0},{2,1},{3,2},{4,3},{5,4},{6,5},{7,6},{0,7},{9,8},{10,9},{11,1... | collective-permute-start | bytes 1443848 | tf_op jit(solution)/shard_map/ppermute | solution.py:79
  97.4 0.8 copy-start.5
  97.5 9.5 %collective-permute-start.2 = (bf16[32,7520]{1,0:T(8,128)(2,1)S(1)}, bf16[32,7520]{1,0:T(8,128)(2,1)}, u32[]{:S(2)}, u32[]{:S(2)}) collective-permute-start(bf16[32,7520]{1,0:T(8,128)(2,1)S(1)} %collective-permute-done.1), channel_id=1, source_target_pairs={{0,1},{1,2},{2,3},{3,4},{4,5},{5,6},{6,7},{7,0},{8,9},{9,10},{10,1... | collective-permute-start | bytes 1443848 | tf_op jit(solution)/shard_map/ppermute | solution.py:76
  98.2 8.9 %collective-permute-start.5 = (bf16[32,7520]{1,0:T(8,128)(2,1)}, bf16[32,7520]{1,0:T(8,128)(2,1)}, u32[]{:S(2)}, u32[]{:S(2)}) collective-permute-start(bf16[32,7520]{1,0:T(8,128)(2,1)} %collective-permute-done.4), channel_id=1, source_target_pairs={{1,0},{2,1},{3,2},{4,3},{5,4},{6,5},{7,6},{0,7},{9,8},{10,9},{11,1... | collective-permute-start | bytes 1443848 | tf_op jit(solution)/shard_map/ppermute | solution.py:79
  106.9 9.7 %collective-permute-start.3 = (bf16[32,7520]{1,0:T(8,128)(2,1)}, bf16[32,7520]{1,0:T(8,128)(2,1)}, u32[]{:S(2)}, u32[]{:S(2)}) collective-permute-start(bf16[32,7520]{1,0:T(8,128)(2,1)} %collective-permute-done.2), channel_id=1, source_target_pairs={{0,1},{1,2},{2,3},{3,4},{4,5},{5,6},{6,7},{7,0},{8,9},{9,10},{10,1... | collective-permute-start | bytes 1443848 | tf_op jit(solution)/shard_map/ppermute | solution.py:76
  107.1 20.4 %collective-permute-start.6 = (bf16[32,7520]{1,0:T(8,128)(2,1)}, bf16[32,7520]{1,0:T(8,128)(2,1)S(1)}, u32[]{:S(2)}, u32[]{:S(2)}) collective-permute-start(bf16[32,7520]{1,0:T(8,128)(2,1)} %collective-permute-done.5), channel_id=1, source_target_pairs={{1,0},{2,1},{3,2},{4,3},{5,4},{6,5},{7,6},{0,7},{9,8},{10,9},{11,1... | collective-permute-start | bytes 1443848 | tf_op jit(solution)/shard_map/ppermute | solution.py:79
  136.1 130.6 %all-reduce.5.cloned.1.call-start = ((), (), s32[]{:S(2)}) async-start(), calls=%async_computation.4 | async-start | bytes 2097152 | tf_op jit(solution)/shard_map/psum | solution.py:111
  137.6 204.9 %reduce-scatter.5.cloned.1.call-start = ((), (), s32[]{:S(2)}) async-start(), calls=%async_computation.2 | async-start | bytes 589824 | tf_op jit(solution)/shard_map/reduce_scatter | solution.py:102
  137.8 6.1 %copy-start.1 = (bf16[8,32,7520]{2,1,0:T(8,128)(2,1)S(1)}, bf16[8,32,7520]{2,1,0:T(8,128)(2,1)}, u32[]{:S(2)}) copy-start(bf16[8,32,7520]{2,1,0:T(8,128)(2,1)} %gather_fusion) | copy-start | bytes 11550724
Sparse Core Ops, SparseCore 0:
  32.5 43.5 reduce-scatter.6
  136.2 81.1 all-reduce.2
  220.6 46.0 all-reduce.4
  270.6 71.8 reduce-scatter.4
